TPU v7x, 32 devices: a whole 2x2x4 slice. The times are simulated.
32 devices in a mesh: dp: 4 (over y, core), fsdp: 8 (over z, x).
Axes of the slice: x: 2, y: 2, z: 4, core: 2. Of those that a mesh axis runs over, the one named last changes fastest.
Arguments:
- tokens: bfloat16 [32768, 768], P(('dp', 'fsdp')), may hold values from -6 to 6
- cotangent: bfloat16 [32768, 768], P(('dp', 'fsdp')), may hold values from -6 to 6
- segment_ids: int32 [64, 512], P(('dp', 'fsdp')), may hold values from 0 to 47, never falling along the last dimension, each value on 1 to 16 neighbouring positions
- w_attn: float32 [768, 2304], P('fsdp'), may hold values from -0.3125 to 0.3125
- moment_attn: float32 [768, 2304], P('fsdp'), may hold values from -543.058 to 543.058
- square_attn: float32 [768, 2304], P('fsdp'), may hold values from 3276.8 to 26214.4
- w_proj: float32 [768, 768], P('fsdp'), may hold values from -0.4375 to 0.4375
- moment_proj: float32 [768, 768], P('fsdp'), may hold values from -543.058 to 543.058
- square_proj: float32 [768, 768], P('fsdp'), may hold values from 3276.8 to 26214.4
- w_up: float32 [768, 3072], P('fsdp'), may hold values from -0.21875 to 0.21875
- moment_up: float32 [768, 3072], P('fsdp'), may hold values from -543.058 to 543.058
- square_up: float32 [768, 3072], P('fsdp'), may hold values from 3276.8 to 26214.4
- w_down: float32 [3072, 768], P('fsdp'), may hold values from -0.15625 to 0.15625
- moment_down: float32 [3072, 768], P('fsdp'), may hold values from -543.058 to 543.058
- square_down: float32 [3072, 768], P('fsdp'), may hold values from 3276.8 to 26214.4
- vectors: float32 [768, 12], P('fsdp'), may hold values from -1.2 to 1.3
- moment_vec: float32 [768, 12], P('fsdp'), may hold values from -905.0967 to 905.0967
- square_vec: float32 [768, 12], P('fsdp'), may hold values from 16384 to 131072
Outputs:
- block_out: bfloat16 [32768, 768], P(('dp', 'fsdp'))
- grad_tokens: float32 [32768, 768], P(('dp', 'fsdp'))
- attn_new: float32 [768, 2304], P('fsdp')
- attn_moment: float32 [768, 2304], P('fsdp')
- attn_square: float32 [768, 2304], P('fsdp')
- proj_new: float32 [768, 768], P('fsdp')
- proj_moment: float32 [768, 768], P('fsdp')
- proj_square: float32 [768, 768], P('fsdp')
- up_new: float32 [768, 3072], P('fsdp')
- up_moment: float32 [768, 3072], P('fsdp')
- up_square: float32 [768, 3072], P('fsdp')
- down_new: float32 [3072, 768], P('fsdp')
- down_moment: float32 [3072, 768], P('fsdp')
- down_square: float32 [3072, 768], P('fsdp')
- vec_new: float32 [768, 12], P('fsdp')
- vec_moment: float32 [768, 12], P('fsdp')
- vec_square: float32 [768, 12], P('fsdp')
Inputs may be any that keep to these rules, and one draw needn't show every extreme that they name: `segment_ids`: ids never fall along a block; each caption holds 1 to 16 rows, one of them exactly 16.
All inputs are finite; a program needn't handle non-finite values.
Results may differ from a plain program's by a relative error of at most 0.012.
The roundings to bfloat16 on the way count: a program that leaves them out, or rounds other values in their place, can miss the bound.
Values may be sent and summed in bfloat16 or wider, within the bound.
No kernel may reach another device: no remote copies, remote signals or barrier semaphores. Data moves between devices by JAX's collectives and lax.ppermute only.
A program may use at most 192 MiB of HBM per device.

v0:
```python
import jax
import jax.numpy as jnp
from jax import lax
from jax.sharding import PartitionSpec as P

D = 768
HEADS = 12
HEAD = 64
FF = 3072
PACK = 512
STEP = 5
eps_norm = 1e-06
beta_one = 0.5
beta_two = 0.5
rate_matrix = 0.03
rate_vector = 0.25
weight_decay = 0.1
eps_adam = 1e-08
masked_score = -1e30


def layer_norm(rows_in, gain_vec, shift_vec):
    row_mean = jnp.mean(rows_in, axis=-1, keepdims=True)
    centered = rows_in - row_mean
    row_var = jnp.mean(centered * centered, axis=-1, keepdims=True)
    return centered * lax.rsqrt(row_var + eps_norm) * gain_vec + shift_vec


def contract_rows(left, right):
    return lax.dot_general(
        left, right, (((0,), (0,)), ((), ())), preferred_element_type=jnp.float32
    )


def contract_cols(left, right):
    return lax.dot_general(
        left, right, (((1,), (1,)), ((), ())), preferred_element_type=jnp.float32
    )


def scores_of(qkv_pack, seg_pack):
    queries = qkv_pack[:, :D].reshape(PACK, HEADS, HEAD)
    key_rows = qkv_pack[:, D : 2 * D].reshape(PACK, HEADS, HEAD)
    values = qkv_pack[:, 2 * D :].reshape(PACK, HEADS, HEAD)
    scores = jnp.einsum(
        "qhd,khd->hqk", queries, key_rows, preferred_element_type=jnp.float32
    ) * HEAD ** (-0.5)
    same_caption = seg_pack[:, None] == seg_pack[None, :]
    scores = jnp.where(same_caption[None], scores, masked_score)
    return (queries, key_rows, values, scores)


def attend(packed):
    qkv_pack, seg_pack = packed
    queries, key_rows, values, scores = scores_of(qkv_pack, seg_pack)
    row_max = jnp.max(scores, axis=-1, keepdims=True)
    exp_scores = jnp.exp(scores - row_max)
    exp_total = jnp.sum(exp_scores, axis=-1, keepdims=True)
    soft_weights = (exp_scores / exp_total).astype(jnp.bfloat16)
    mixed_pack = jnp.einsum(
        "hqk,khd->qhd", soft_weights, values, preferred_element_type=jnp.float32
    )
    return (
        mixed_pack.reshape(PACK, D).astype(jnp.bfloat16),
        (row_max + jnp.log(exp_total))[..., 0],
    )


def attend_back(packed):
    qkv_pack, seg_pack, log_total, grad_pack = packed
    queries, key_rows, values, scores = scores_of(qkv_pack, seg_pack)
    soft_exact = jnp.exp(scores - log_total[..., None])
    grad_heads = grad_pack.reshape(PACK, HEADS, HEAD)
    grad_soft = jnp.einsum("qhd,khd->hqk", grad_heads, values, preferred_element_type=jnp.float32)
    row_delta = jnp.sum(soft_exact * grad_soft, axis=-1, keepdims=True)
    grad_score = (soft_exact * (grad_soft - row_delta)).astype(jnp.bfloat16)
    score_scale = HEAD ** (-0.5)
    grad_queries = (
        jnp.einsum("hqk,khd->qhd", grad_score, key_rows, preferred_element_type=jnp.float32)
        * score_scale
    )
    grad_keys = (
        jnp.einsum("hqk,qhd->khd", grad_score, queries, preferred_element_type=jnp.float32)
        * score_scale
    )
    grad_values = jnp.einsum(
        "hqk,qhd->khd",
        soft_exact.astype(jnp.bfloat16),
        grad_heads,
        preferred_element_type=jnp.float32,
    )
    joined = jnp.concatenate(
        [grad_queries.reshape(PACK, D), grad_keys.reshape(PACK, D), grad_values.reshape(PACK, D)],
        axis=1,
    )
    return joined.astype(jnp.bfloat16)


def adam_step(master, moment, square, gradient, rate, decay_rate):
    moment_new = beta_one * moment + (1.0 - beta_one) * gradient
    square_new = beta_two * square + (1.0 - beta_two) * gradient * gradient
    moment_hat = moment_new / (1.0 - beta_one**STEP)
    square_hat = square_new / (1.0 - beta_two**STEP)
    master_new = master - rate * (
        moment_hat / (jnp.sqrt(square_hat) + eps_adam) + decay_rate * master
    )
    return (master_new, moment_new, square_new)


def body(
    tokens,
    cotangent,
    segment_ids,
    w_attn,
    moment_attn,
    square_attn,
    w_proj,
    moment_proj,
    square_proj,
    w_up,
    moment_up,
    square_up,
    w_down,
    moment_down,
    square_down,
    vectors,
    moment_vec,
    square_vec,
):
    low_attn = w_attn.astype(jnp.bfloat16)
    low_proj = w_proj.astype(jnp.bfloat16)
    low_up = w_up.astype(jnp.bfloat16)
    low_down = w_down.astype(jnp.bfloat16)
    low_vec = vectors.astype(jnp.bfloat16)
    full_attn, full_proj, full_up, full_down, full_vec = (
        lax.all_gather(low_attn, "fsdp", axis=0, tiled=True),
        lax.all_gather(low_proj, "fsdp", axis=0, tiled=True),
        lax.all_gather(low_up, "fsdp", axis=0, tiled=True),
        lax.all_gather(low_down, "fsdp", axis=0, tiled=True),
        lax.all_gather(low_vec, "fsdp", axis=0, tiled=True),
    )
    vec_full = full_vec.astype(jnp.float32)
    gain_one = vec_full[:, 0]
    shift_one = vec_full[:, 1]
    q_bias = vec_full[:, 2]
    v_bias = vec_full[:, 3]
    out_bias = vec_full[:, 4]
    gain_two = vec_full[:, 5]
    shift_two = vec_full[:, 6]
    down_bias = vec_full[:, 7]
    up_bias = vec_full[:, 8:12].T.reshape(FF)
    row_count = tokens.shape[0]
    pack_count = row_count // PACK
    inputs = tokens.astype(jnp.float32)
    normed_one = layer_norm(inputs, gain_one, shift_one).astype(jnp.bfloat16)
    qkv_bias = jnp.concatenate([q_bias, jnp.zeros_like(q_bias), v_bias])
    qkv = (jnp.dot(normed_one, full_attn, preferred_element_type=jnp.float32) + qkv_bias).astype(
        jnp.bfloat16
    )
    qkv_packs = qkv.reshape(pack_count, PACK, 3 * D)
    mixed_rows, log_total = lax.map(attend, (qkv_packs, segment_ids))
    mixed_rows = mixed_rows.reshape(row_count, D)
    residual = (
        inputs + jnp.dot(mixed_rows, full_proj, preferred_element_type=jnp.float32) + out_bias
    )
    normed_two = layer_norm(residual, gain_two, shift_two).astype(jnp.bfloat16)
    pre_act = jnp.dot(normed_two, full_up, preferred_element_type=jnp.float32) + up_bias
    activated = jax.nn.gelu(pre_act).astype(jnp.bfloat16)
    output = (
        residual + jnp.dot(activated, full_down, preferred_element_type=jnp.float32) + down_bias
    )
    back_attn, back_proj, back_up, back_down = (
        lax.all_gather(low_attn, "fsdp", axis=0, tiled=True),
        lax.all_gather(low_proj, "fsdp", axis=0, tiled=True),
        lax.all_gather(low_up, "fsdp", axis=0, tiled=True),
        lax.all_gather(low_down, "fsdp", axis=0, tiled=True),
    )
    grad_rows = cotangent.astype(jnp.float32)
    grad_down = contract_rows(activated, cotangent)
    grad_down_bias = jnp.sum(grad_rows, axis=0)
    grad_act = contract_cols(cotangent, back_down)
    gelu_value, gelu_pull = jax.vjp(jax.nn.gelu, pre_act)
    grad_pre = gelu_pull(grad_act)[0].astype(jnp.bfloat16)
    grad_up = contract_rows(normed_two, grad_pre)
    grad_up_bias = jnp.sum(grad_pre.astype(jnp.float32), axis=0)
    grad_normed_two = contract_cols(grad_pre, back_up)
    norm_value, second_pull = jax.vjp(layer_norm, residual, gain_two, shift_two)
    grad_resid_part, grad_gain_two, grad_shift_two = second_pull(grad_normed_two)
    grad_resid = grad_rows + grad_resid_part
    sum_up, sum_down = (
        lax.psum_scatter(grad_up, "fsdp", scatter_dimension=0, tiled=True),
        lax.psum_scatter(grad_down, "fsdp", scatter_dimension=0, tiled=True),
    )
    grad_branch = grad_resid.astype(jnp.bfloat16)
    grad_proj = contract_rows(mixed_rows, grad_branch)
    grad_out_bias = jnp.sum(grad_branch.astype(jnp.float32), axis=0)
    grad_mixed = contract_cols(grad_branch, back_proj).astype(jnp.bfloat16)
    grad_qkv = lax.map(
        attend_back, (qkv_packs, segment_ids, log_total, grad_mixed.reshape(pack_count, PACK, D))
    )
    grad_qkv = grad_qkv.reshape(row_count, 3 * D)
    grad_attn = contract_rows(normed_one, grad_qkv)
    qkv_bias_grad = jnp.sum(grad_qkv.astype(jnp.float32), axis=0)
    grad_normed_one = contract_cols(grad_qkv, back_attn)
    first_value, first_pull = jax.vjp(layer_norm, inputs, gain_one, shift_one)
    grad_in_part, grad_gain_one, grad_shift_one = first_pull(grad_normed_one)
    grad_inputs = grad_resid + grad_in_part
    grad_columns = jnp.stack(
        [
            grad_gain_one,
            grad_shift_one,
            qkv_bias_grad[:D],
            qkv_bias_grad[2 * D :],
            grad_out_bias,
            grad_gain_two,
            grad_shift_two,
            grad_down_bias,
        ],
        axis=1,
    )
    grad_vec = jnp.concatenate([grad_columns, grad_up_bias.reshape(4, D).T], axis=1)
    sum_attn, sum_proj, sum_vec = (
        lax.psum_scatter(grad_attn, "fsdp", scatter_dimension=0, tiled=True),
        lax.psum_scatter(grad_proj, "fsdp", scatter_dimension=0, tiled=True),
        lax.psum_scatter(grad_vec, "fsdp", scatter_dimension=0, tiled=True),
    )
    total_attn, total_proj, total_up, total_down, total_vec = lax.psum(
        (sum_attn, sum_proj, sum_up, sum_down, sum_vec), "dp"
    )
    attn_upd = adam_step(w_attn, moment_attn, square_attn, total_attn, rate_matrix, weight_decay)
    proj_upd = adam_step(w_proj, moment_proj, square_proj, total_proj, rate_matrix, weight_decay)
    up_upd = adam_step(w_up, moment_up, square_up, total_up, rate_matrix, weight_decay)
    down_upd = adam_step(w_down, moment_down, square_down, total_down, rate_matrix, weight_decay)
    vec_upd = adam_step(vectors, moment_vec, square_vec, total_vec, rate_vector, 0.0)
    return (
        output.astype(jnp.bfloat16),
        grad_inputs,
        attn_upd[0],
        attn_upd[1],
        attn_upd[2],
        proj_upd[0],
        proj_upd[1],
        proj_upd[2],
        up_upd[0],
        up_upd[1],
        up_upd[2],
        down_upd[0],
        down_upd[1],
        down_upd[2],
        vec_upd[0],
        vec_upd[1],
        vec_upd[2],
    )


def solution(mesh):
    in_specs = (
        P(("dp", "fsdp"), None),
        P(("dp", "fsdp"), None),
        P(("dp", "fsdp"), None),
        P("fsdp", None),
        P("fsdp", None),
        P("fsdp", None),
        P("fsdp", None),
        P("fsdp", None),
        P("fsdp", None),
        P("fsdp", None),
        P("fsdp", None),
        P("fsdp", None),
        P("fsdp", None),
        P("fsdp", None),
        P("fsdp", None),
        P("fsdp", None),
        P("fsdp", None),
        P("fsdp", None),
    )
    out_specs = (
        P(("dp", "fsdp"), None),
        P(("dp", "fsdp"), None),
        P("fsdp", None),
        P("fsdp", None),
        P("fsdp", None),
        P("fsdp", None),
        P("fsdp", None),
        P("fsdp", None),
        P("fsdp", None),
        P("fsdp", None),
        P("fsdp", None),
        P("fsdp", None),
        P("fsdp", None),
        P("fsdp", None),
        P("fsdp", None),
        P("fsdp", None),
        P("fsdp", None),
    )
    return jax.shard_map(body, mesh=mesh, in_specs=in_specs, out_specs=out_specs, check_vma=False)
```

profile of v0, /device:TPU:0, one launch (start us, length us, event | category | flops | bytes accessed | tf_op | source)
XLA Modules:
  0.0 1021.2 jit_solution(2336385018633477261)
XLA Ops:
  13.1 33.0 %all-gather = bf16[8,96,12]{1,2,0:T(8,128)(2,1)S(1)} all-gather(bf16[1,96,12]{1,2,0:T(8,128)(2,1)S(1)} %convert_bitcast_fusion), channel_id=1, replica_groups=mesh['dp'=4,'fsdp'=8] {'fsdp'}, dimensions={0}, use_global_device_ids=true | all-gather | bytes 20736 | tf_op jit(solution)/shard_map/all_gather | solution.py:140
  52.6 25.7 %all-gather.6.cloned.1.call-done = bf16[768,2304]{1,0:T(8,128)(2,1)} async-done(((bf16[96,2304]{1,0:T(8,128)(2,1)}), bf16[768,2304]{1,0:T(8,128)(2,1)}) %all-gather.6.cloned.1.call-update) | async-done | bytes 3538960 | tf_op jit(solution)/shard_map/all_gather | solution.py:136
  78.3 7.7 add_convert_fusion
  92.8 27.6 %while.22 = (s32[]{:T(128)}, bf16[2,512,768]{2,1,0:T(8,128)(2,1)}, f32[2,12,512]{2,1,0:T(8,128)S(1)}, bf16[2,512,2304]{1,2,0:T(8,128)(2,1)}, s32[2,512]{1,0:T(2,128)S(1)}, /*index=5*/s32[]{:T(128)}) while((s32[]{:T(128)}, bf16[2,512,768]{2,1,0:T(8,128)(2,1)}, f32[2,12,512]{2,1,0:T(8,128)S(1)}, bf16[2,512,2304]{1,2,0:T(8,128)(2,1)}, ...), condition=%wide.region_5.6_spmd, body=%wide.region_2.5_spmd.sunk | while | flops 843704320 | bytes 54753372 | solution.py:161
  128.3 73.5 %all-gather.10.cloned.1.call-done = bf16[768,3072]{1,0:T(8,128)(2,1)} async-done(((bf16[96,3072]{1,0:T(8,128)(2,1)}), bf16[768,3072]{1,0:T(8,128)(2,1)}) %all-gather.10.cloned.1.call-update) | async-done | bytes 4718608 | tf_op jit(solution)/shard_map/all_gather | solution.py:138
  201.8 11.2 %fusion.47 = f32[1024,3072]{1,0:T(8,128)} fusion(bf16[768,3072]{1,0:T(8,128)(2,1)} %all-gather.10.cloned.1.call-done, f32[1024,768]{0,1:T(8,128)} %get-tuple-element.264, f32[768]{0:T(1024)S(1)} %copy-done.28, f32[768]{0:T(1024)S(1)} %copy-done.24, f32[1024]{0:T(1024)S(1)} %fusion.42, f32[1024]{0:T(1024)S(1)} %broadcast_multiply_fusion), kind=kOutput, calls=%fused_computation.117 | convolution fusion | flops 4835770368 | bytes 20461568 | tf_op jit(solution)/shard_map/dot_general | solution.py:167
  213.0 69.1 %all-gather.12.cloned.1.call-done = bf16[3072,768]{1,0:T(8,128)(2,1)} async-done(((bf16[384,768]{1,0:T(8,128)(2,1)}), bf16[3072,768]{1,0:T(8,128)(2,1)}) %all-gather.12.cloned.1.call-update) | async-done | bytes 4718608 | tf_op jit(solution)/shard_map/all_gather | solution.py:139
  282.1 15.5 %convert_reduce_fusion = (f32[3072]{0:T(1024)}, bf16[1024,3072]{1,0:T(8,128)(2,1)S(1)}) fusion(f32[1024,3072]{1,0:T(8,128)} %fusion.47, f32[3072]{0:T(1024)S(1)} %copy-done.45, bf16[1024,768]{1,0:T(8,128)(2,1)S(1)} %copy-done.13, bf16[3072,768]{1,0:T(8,128)(2,1)} %all-gather.12.cloned.1.call-done), kind=kOutput, calls=%fused_computation.40 | convolution fusion | flops 4904186880 | bytes 25190400 | tf_op jit(solution)/shard_map/dot_general | solution.py:36
  297.6 7.3 fusion.61
  304.9 13.8 %copy.99 = f32[1024,768]{0,1:T(8,128)S(1)} copy(f32[1024,768]{1,0:T(8,128)} %get-tuple-element.268) | data formatting | bytes 6291456 | tf_op jit(solution)/shard_map/dot_general | solution.py:36
  333.2 52.4 %while.23 = (s32[]{:T(128)}, bf16[2,512,2304]{1,2,0:T(8,128)(2,1)}, bf16[2,512,2304]{1,2,0:T(8,128)(2,1)}, s32[2,512]{1,0:T(2,128)S(1)}, f32[2,12,512]{2,1,0:T(8...) while((s32[]{:T(128)}, bf16[2,512,2304]{1,2,0:T(8,128)(2,1)}, bf16[2,512,2304]{1,2,0:T(8,128)(2,1)}, ...), condition=%wide.region_12.13_spmd, body=%wide.region_10.12_spmd.sunk | while | flops 2069751808 | bytes 120764512 | solution.py:198
  347.6 7.1 multiply_convert_fusion.9
  373.8 7.0 multiply_convert_fusion.9
  385.6 6.9 copy.102
  392.5 8.7 fusion.43
  402.6 13.0 %fusion.48 = f32[3072,768]{1,0:T(8,128)} fusion(bf16[1024,768]{1,0:T(8,128)(2,1)S(1)} %copy-done.14, f32[1024,3072]{1,0:T(8,128)} %fusion.47, f32[3072]{0:T(1024)S(1)} %copy-done.46), kind=kOutput, calls=%fused_computation.118 | convolution fusion | flops 4863295488 | bytes 23605248 | tf_op jit(solution)/shard_map/dot_general | solution.py:30
  416.3 10.6 %fusion.46 = f32[768,3072]{1,0:T(8,128)} fusion(bf16[1024,3072]{1,0:T(8,128)(2,1)} %copy-done.57, f32[1024,768]{0,1:T(8,128)} %get-tuple-element.264, f32[768]{0:T(1024)S(1)} %copy-done.29, f32[768]{0:T(1024)S(1)} %copy-done.25, f32[1024]{0:T(1024)S(1)} %copy-done.27, f32[1024]{0:T(1024)S(1)} %copy-done.23), kind=kOutput, calls=%fused_computation.116 | convolution fusion | flops 4835770368 | bytes 18888704 | tf_op jit(solution)/shard_map/dot_general | solution.py:30
  431.1 7.9 fusion.60
  452.4 78.3 %reduce-scatter.8.cloned.1.call-done = f32[96,2304]{1,0:T(8,128)} async-done(((f32[768,2304]{1,0:T(8,128)}), f32[96,2304]{1,0:T(8,128)}) %reduce-scatter.8.cloned.1.call-update) | async-done | bytes 884752 | tf_op jit(solution)/shard_map/reduce_scatter | solution.py:223
  530.7 164.9 %reduce-scatter.14.cloned.1.call-done = f32[384,768]{1,0:T(8,128)} async-done(((f32[3072,768]{1,0:T(8,128)}), f32[384,768]{1,0:T(8,128)}) %reduce-scatter.14.cloned.1.call-update) | async-done | bytes 1179664 | tf_op jit(solution)/shard_map/reduce_scatter | solution.py:192
  695.5 164.8 %reduce-scatter.12.cloned.1.call-done = f32[96,3072]{1,0:T(8,128)} async-done(((f32[768,3072]{1,0:T(8,128)}), f32[96,3072]{1,0:T(8,128)}) %reduce-scatter.12.cloned.1.call-update) | async-done | bytes 1179664 | tf_op jit(solution)/shard_map/reduce_scatter | solution.py:191
  860.4 12.3 %add_convert_fusion.1 = bf16[1024,768]{0,1:T(8,128)(2,1)} fusion(f32[1024,768]{0,1:T(8,128)} %get-tuple-element.264, bf16[3072,768]{1,0:T(8,128)(2,1)} %all-gather.12.cloned.1.call-done, f32[768]{0:T(1024)S(1)} %copy-done.50, f32[1024,3072]{1,0:T(8,128)} %fusion.47, f32[3072]{0:T(1024)S(1)} %copy-done.46), kind=kOutput, calls=%fused_computation.67 | convolution fusion | flops 4865654784 | bytes 22035456 | tf_op jit(solution)/shard_map/dot_general | solution.py:170
  877.8 47.6 %reduce-scatter.16.cloned.1.call-done = f32[96,12]{1,0:T(8,128)} async-done(((f32[768,12]{1,0:T(8,128)}), f32[96,12]{1,0:T(8,128)}) %reduce-scatter.16.cloned.1.call-update) | async-done | bytes 4624
  932.9 69.0 %all-reduce.3.cloned.1.call-done = (f32[96,2304]{1,0:T(8,128)}, f32[96,768]{1,0:T(8,128)}, f32[96,3072]{1,0:T(8,128)}, f32[384,768]{1,0:T(8,128)}) async-done(((f32[96,2304]{1,0:T(8,128)}, f32[96,768]{1,0:T(8,128)}, f32[96,3072]{1,0:T(8,128)}, f32[384,768]{1,0:T(8,128)}), (f32[96,2304]{1,0:T(8,128)}, f32[96,768]{1,0:T(8,128)}, f32[96,3072]{1,0:T(8,128)}, f32[384,768]{1,0:T(8,128)})) %all-reduce.3.cloned.1.call-update) | async-done | bytes 3538960 | tf_op jit(solution)/shard_map/psum | solution.py:227
  (245 shorter events, 150.9 us)
Async XLA Ops:
  7.2 71.1 %all-gather.6.cloned.1.call-start = ((), (), s32[]{:S(2)}) async-start(), calls=%async_computation.5 | async-start | bytes 3981312 | tf_op jit(solution)/shard_map/all_gather | solution.py:136
  9.4 111.6 %all-gather.8.cloned.1.call-start = ((), (), s32[]{:S(2)}) async-start(), calls=%async_computation.6 | async-start | bytes 1327104 | tf_op jit(solution)/shard_map/all_gather | solution.py:137
  11.1 190.7 %all-gather.10.cloned.1.call-start = ((), (), s32[]{:S(2)}) async-start(), calls=%async_computation.7 | async-start | bytes 5308416 | tf_op jit(solution)/shard_map/all_gather | solution.py:138
  12.1 270.0 %all-gather.12.cloned.1.call-start = ((), (), s32[]{:S(2)}) async-start(), calls=%async_computation.8 | async-start | bytes 5308416 | tf_op jit(solution)/shard_map/all_gather | solution.py:139
  13.1 439.3 %reduce-scatter.10.cloned.1.call-start = ((), (), s32[]{:S(2)}) async-start(), calls=%async_computation.10 | async-start | bytes 2654208 | tf_op jit(solution)/shard_map/reduce_scatter | solution.py:224
  49.2 71.8 %copy-start = (bf16[1024,768]{0,1:T(8,128)(2,1)}, bf16[1024,768]{0,1:T(8,128)(2,1)S(1)}, u32[]{:S(2)}) copy-start(bf16[1024,768]{0,1:T(8,128)(2,1)S(1)} %copy.93) | copy-start | bytes 4718596
  49.5 36.6 %copy-start.30 = (f32[1024]{0:T(1024)}, f32[1024]{0:T(1024)S(1)}, u32[]{:S(2)}) copy-start(f32[1024]{0:T(1024)S(1)} %broadcast_multiply_fusion.1) | copy-start | bytes 12292
  50.0 36.1 %copy-start.39 = (f32[1024]{0:T(1024)}, f32[1024]{0:T(1024)S(1)}, u32[]{:S(2)}) copy-start(f32[1024]{0:T(1024)S(1)} %fusion.31) | copy-start | bytes 12292
  126.0 75.8 %copy-start.24 = (f32[768]{0:T(1024)S(1)}, f32[768]{0:T(1024)}, u32[]{:S(2)}) copy-start(f32[768]{0:T(1024)} %get-tuple-element.196) | copy-start | bytes 9220
  126.0 75.8 %copy-start.28 = (f32[768]{0:T(1024)S(1)}, f32[768]{0:T(1024)}, u32[]{:S(2)}) copy-start(f32[768]{0:T(1024)} %get-tuple-element.198) | copy-start | bytes 9220
  126.0 196.1 %copy-start.22 = (f32[1024]{0:T(1024)}, f32[1024]{0:T(1024)S(1)}, u32[]{:S(2)}) copy-start(f32[1024]{0:T(1024)S(1)} %broadcast_multiply_fusion) | copy-start | bytes 12292
  128.2 193.9 %copy-start.26 = (f32[1024]{0:T(1024)}, f32[1024]{0:T(1024)S(1)}, u32[]{:S(2)}) copy-start(f32[1024]{0:T(1024)S(1)} %fusion.42) | copy-start | bytes 12292
  201.8 80.3 %copy-start.13 = (bf16[1024,768]{1,0:T(8,128)(2,1)S(1)}, bf16[1024,768]{1,0:T(8,128)(2,1)}, u32[]{:S(2)}) copy-start(bf16[1024,768]{1,0:T(8,128)(2,1)} %param.23) | copy-start | bytes 4718596
  201.8 80.3 %copy-start.45 = (f32[3072]{0:T(1024)S(1)}, f32[3072]{0:T(1024)}, u32[]{:S(2)}) copy-start(f32[3072]{0:T(1024)} %add.231) | copy-start | bytes 36868
  330.4 200.3 %reduce-scatter.8.cloned.1.call-start = ((), (), s32[]{:S(2)}) async-start(), calls=%async_computation.9 | async-start | bytes 7962624 | tf_op jit(solution)/shard_map/reduce_scatter | solution.py:223
  401.2 294.3 %reduce-scatter.14.cloned.1.call-start = ((), (), s32[]{:S(2)}) async-start(), calls=%async_computation.12 | async-start | bytes 10616832 | tf_op jit(solution)/shard_map/reduce_scatter | solution.py:192
  415.6 444.7 %reduce-scatter.12.cloned.1.call-start = ((), (), s32[]{:S(2)}) async-start(), calls=%async_computation.11 | async-start | bytes 10616832 | tf_op jit(solution)/shard_map/reduce_scatter | solution.py:191
  426.9 498.5 %reduce-scatter.16.cloned.1.call-start = ((), (), s32[]{:S(2)}) async-start(), calls=%async_computation.13 | async-start | bytes 442368
  451.3 409.1 %copy-start.50 = (f32[768]{0:T(1024)S(1)}, f32[768]{0:T(1024)}, u32[]{:S(2)}) copy-start(f32[768]{0:T(1024)} %get-tuple-element.197) | copy-start | bytes 9220
  452.3 549.6 %all-reduce.3.cloned.1.call-start = ((), (), s32[]{:S(2)}) async-start(), calls=%async_computation.14 | async-start | bytes 7077888 | tf_op jit(solution)/shard_map/psum | solution.py:227
  875.4 56.8 %copy-start.42 = (f32[96,12]{0,1:T(8,128)S(1)}, f32[96,12]{0,1:T(8,128)}, u32[]{:S(2)}) copy-start(f32[96,12]{0,1:T(8,128)} %param.37) | copy-start | bytes 13828
  875.4 56.8 %copy-start.48 = (f32[96,12]{0,1:T(8,128)S(1)}, f32[96,12]{0,1:T(8,128)}, u32[]{:S(2)}) copy-start(f32[96,12]{0,1:T(8,128)} %param.38) | copy-start | bytes 13828
  875.4 56.8 %copy-start.49 = (f32[96,12]{0,1:T(8,128)S(1)}, f32[96,12]{0,1:T(8,128)}, u32[]{:S(2)}) copy-start(f32[96,12]{0,1:T(8,128)} %param.39) | copy-start | bytes 13828
  875.4 126.4 %copy-start.15 = (f32[96,768]{1,0:T(8,128)S(1)}, f32[96,768]{1,0:T(8,128)}, u32[]{:S(2)}) copy-start(f32[96,768]{1,0:T(8,128)} %param.28) | copy-start | bytes 884740
  (44 other events, 267.8 us)
Sparse Core Ops, SparseCore 0:
  10.8 67.4 all-gather.5
  81.1 39.8 all-gather.7
  123.7 77.9 all-gather.9
  204.4 77.6 all-gather.11
  330.5 68.1 reduce-scatter.9
  402.3 128.3 reduce-scatter.7
  534.3 161.2 reduce-scatter.13
  699.1 161.1 reduce-scatter.11
  864.2 61.1 reduce-scatter.15
  927.9 73.9 all-reduce.2
where the time goes:
time: 1030 us; the launch traced here: 1020 us
  waiting for transfers between devices  694 us (67%)
  matrix products  147 us (14%)
  local copies, waits for them, and re-layouts  64 us (6%)
  other arithmetic  61.3 us (6%)
  blocking collectives  38.9 us (4%)
  between operations  14.9 us (1%)
    reduce_scatter x1, waiting for transfers between devices, body(): lax.psum_scatter(grad_down, 'fsdp', scatter_dimension=0, tiled=True)  165 us
    reduce_scatter x1, waiting for transfers between devices, body(): lax.psum_scatter(grad_up, 'fsdp', scatter_dimension=0, tiled=True)  165 us
    reduce_scatter x1, waiting for transfers between devices, body(): lax.psum_scatter(grad_attn, 'fsdp', scatter_dimension=0, tiled=True)  78.3 us
    all_gather x1, waiting for transfers between devices, body(): lax.all_gather(low_up, 'fsdp', axis=0, tiled=True)  73.5 us
    all_gather x1, waiting for transfers between devices, body(): lax.all_gather(low_down, 'fsdp', axis=0, tiled=True)  69.1 us
    psum x1, waiting for transfers between devices, body(): lax.psum((sum_attn, sum_proj, sum_up, sum_down, sum_vec), 'dp')  69 us
    unnamed x11, waiting for transfers between devices  47.8 us
    dot_general x4, matrix products, contract_rows(): lax.dot_general(left, right, (((0,), (0,)), ((), ())), preferred_element_...  35.1 us
  transfers between devices with their start and end apart: 10, of which 9 were waited for; matrix products, arithmetic and copies ran while one was open for 20% of the time, Pallas kernels for 0%

commit v1 on v0

--- a/solution.py
+++ b/solution.py
@@ -17,6 +17,22 @@
 weight_decay = 0.1
 eps_adam = 1e-08
 masked_score = -1e30
+
+
+def gather_around(x, axis, dim):
+    ways, here, step = (lax.axis_size(axis), lax.axis_index(axis), x.shape[dim])
+    dims = [n * ways if d == dim else n for d, n in enumerate(x.shape)]
+    full = lax.dynamic_update_slice_in_dim(jnp.zeros(dims, x.dtype), x, here * step, axis=dim)
+    going_up = going_down = x
+    for far in range(1, ways // 2 + 1):
+        going_up = lax.ppermute(going_up, axis, [(d, (d + 1) % ways) for d in range(ways)])
+        full = lax.dynamic_update_slice_in_dim(full, going_up, (here - far) % ways * step, axis=dim)
+        if 2 * far < ways:
+            going_down = lax.ppermute(going_down, axis, [(d, (d - 1) % ways) for d in range(ways)])
+            full = lax.dynamic_update_slice_in_dim(
+                full, going_down, (here + far) % ways * step, axis=dim
+            )
+    return full
 
 
 def layer_norm(rows_in, gain_vec, shift_vec):
@@ -137,7 +153,7 @@
         lax.all_gather(low_proj, "fsdp", axis=0, tiled=True),
         lax.all_gather(low_up, "fsdp", axis=0, tiled=True),
         lax.all_gather(low_down, "fsdp", axis=0, tiled=True),
-        lax.all_gather(low_vec, "fsdp", axis=0, tiled=True),
+        gather_around(low_vec, "fsdp", 0),
     )
     vec_full = full_vec.astype(jnp.float32)
     gain_one = vec_full[:, 0]

time: 1030 us -> 1030 us (level)
  blocking collectives: 38.9 us -> 5.75 us
  waiting for transfers between devices: 694 us -> 721 us
  starting transfers between devices: 0.42 us -> 16 us
    all_gather x1 -> x0, blocking collectives: 33 us -> none  [body(): lax.all_gather(low_vec, 'fsdp', axis=0, tiled=True)]
    ppermute x0 -> x7, starting transfers between devices: none -> 15.6 us  [the longest x3 15.6 us: gather_around(): lax.ppermute(going_down, axis, [(d, (d - 1) % ways) for d in range(ways)])]
    unnamed x11, waiting for transfers between devices: 47.8 us -> 59.9 us
    dot_general x2, local copies, waits for them, and re-layouts: 17.8 us -> 7.35 us  [contract_cols(): lax.dot_general(left, right, (((1,), (1,)), ((), ())), preferred_element_...]
  transfers between devices with their start and end apart: 10 -> 17, of which waited for: 9 -> 13; matrix products, arithmetic and copies ran while one was open for 20% -> 19% of each run, Pallas kernels for 0% -> 0%
where the time goes in v1:
time: 1030 us; the launch traced here: 1020 us
  waiting for transfers between devices  721 us (70%)
  matrix products  146 us (14%)
  local copies, waits for them, and re-layouts  57.3 us (6%)
  other arithmetic  56.8 us (6%)
  starting transfers between devices  16 us (2%)
  between operations  15.3 us (1%)
    reduce_scatter x1, waiting for transfers between devices, body(): lax.psum_scatter(grad_up, 'fsdp', scatter_dimension=0, tiled=True)  165 us
    reduce_scatter x1, waiting for transfers between devices, body(): lax.psum_scatter(grad_down, 'fsdp', scatter_dimension=0, tiled=True)  165 us
    reduce_scatter x1, waiting for transfers between devices, body(): lax.psum_scatter(grad_attn, 'fsdp', scatter_dimension=0, tiled=True)  80.8 us
    all_gather x1, waiting for transfers between devices, body(): lax.all_gather(low_up, 'fsdp', axis=0, tiled=True)  75.4 us
    psum x1, waiting for transfers between devices, body(): lax.psum((sum_attn, sum_proj, sum_up, sum_down, sum_vec), 'dp')  69.2 us
    all_gather x1, waiting for transfers between devices, body(): lax.all_gather(low_down, 'fsdp', axis=0, tiled=True)  64.4 us
    unnamed x11, waiting for transfers between devices  59.9 us
    dot_general x4, matrix products, contract_cols(): lax.dot_general(left, right, (((1,), (1,)), ((), ())), preferred_element_...  33.4 us
  transfers between devices with their start and end apart: 17, of which 13 were waited for; matrix products, arithmetic and copies ran while one was open for 19% of the time, Pallas kernels for 0%

profile of v1, /device:TPU:0, one launch (start us, length us, event | category | flops | bytes accessed | tf_op | source)
XLA Modules:
  0.0 1019.2 jit_solution(11269909110236448289)
XLA Ops:
  45.4 33.0 %all-gather.5.cloned.1.call-done = bf16[768,2304]{1,0:T(8,128)(2,1)} async-done(((bf16[96,2304]{1,0:T(8,128)(2,1)}), bf16[768,2304]{1,0:T(8,128)(2,1)}) %all-gather.5.cloned.1.call-update) | async-done | bytes 3538960 | tf_op jit(solution)/shard_map/all_gather | solution.py:152
  78.4 7.8 add_convert_fusion
  92.8 27.6 %while.22 = (s32[]{:T(128)}, bf16[2,512,768]{2,1,0:T(8,128)(2,1)}, f32[2,12,512]{2,1,0:T(8,128)S(1)}, bf16[2,512,2304]{1,2,0:T(8,128)(2,1)}, s32[2,512]{1,0:T(2,128)S(1)}, /*index=5*/s32[]{:T(128)}) while((s32[]{:T(128)}, bf16[2,512,768]{2,1,0:T(8,128)(2,1)}, f32[2,12,512]{2,1,0:T(8,128)S(1)}, bf16[2,512,2304]{1,2,0:T(8,128)(2,1)}, ...), condition=%wide.region_5.6_spmd, body=%wide.region_2.5_spmd.sunk | while | flops 843704320 | bytes 54753372 | solution.py:177
  126.5 75.4 %all-gather.9.cloned.1.call-done = bf16[768,3072]{1,0:T(8,128)(2,1)} async-done(((bf16[96,3072]{1,0:T(8,128)(2,1)}), bf16[768,3072]{1,0:T(8,128)(2,1)}) %all-gather.9.cloned.1.call-update) | async-done | bytes 4718608 | tf_op jit(solution)/shard_map/all_gather | solution.py:154
  201.9 15.9 %multiply_convert_fusion.3 = (bf16[1024,3072]{1,0:T(8,128)(2,1)}, f32[1024,3072]{1,0:T(8,128)}) fusion(f32[3072]{0:T(1024)S(1)} %copy-done.46, bf16[768,3072]{1,0:T(8,128)(2,1)} %all-gather.9.cloned.1.call-done, f32[1024,768]{0,1:T(8,128)} %copy-done.7, f32[768]{0:T(1024)S(1)} %copy-done.49, f32[768]{0:T(1024)S(1)} %copy-done.40, f32[1024]{0:T(1024)S(1)} %fusion.42, ...), kind=kOutput, calls=%fused_computation.41 | convolution fusion | flops 4867227648 | bytes 26765312 | tf_op jit(solution)/shard_map/dot_general | solution.py:183
  217.8 64.4 %all-gather.11.cloned.1.call-done = bf16[3072,768]{1,0:T(8,128)(2,1)} async-done(((bf16[384,768]{1,0:T(8,128)(2,1)}), bf16[3072,768]{1,0:T(8,128)(2,1)}) %all-gather.11.cloned.1.call-update) | async-done | bytes 4718608 | tf_op jit(solution)/shard_map/all_gather | solution.py:155
  282.2 15.5 %convert_reduce_fusion = (f32[3072]{0:T(1024)}, bf16[1024,3072]{1,0:T(8,128)(2,1)S(1)}) fusion(f32[1024,3072]{1,0:T(8,128)} %get-tuple-element.239, f32[3072]{0:T(1024)S(1)} %copy-done.46, bf16[1024,768]{1,0:T(8,128)(2,1)S(1)} %copy-done.15, bf16[3072,768]{1,0:T(8,128)(2,1)} %all-gather.11.cloned.1.call-done), kind=kOutput, calls=%fused_computation.40 | convolution fusion | flops 4904186880 | bytes 25190400 | tf_op jit(solution)/shard_map/dot_general | solution.py:52
  297.7 7.3 fusion.61
  312.3 10.5 %fusion.54 = (f32[1024]{0:T(1024)S(1)}, f32[1024,768]{0,1:T(8,128)S(1)}, bf16[1024,768]{0,1:T(8,128)(2,1)}) fusion(f32[1024]{0:T(1024)S(1)} %multiply_multiply_fusion.8, f32[1024,768]{0,1:T(8,128)S(1)} %copy-done.8, f32[1024]{0:T(1024)S(1)} %broadcast_multiply_fusion, f32[1024]{0:T(1024)S(1)} %fusion.42, f32[1024,768]{0,1:T(8,128)S(1)} %copy-done.10, ...), kind=kOutput, calls=%fused_computation.116 | convolution fusion | flops 4839701504 | bytes 22042624 | tf_op jit(solution)/shard_map/dot_general | solution.py:186
  331.0 52.6 %while.23 = (s32[]{:T(128)}, bf16[2,512,2304]{1,2,0:T(8,128)(2,1)}, bf16[2,512,2304]{1,2,0:T(8,128)(2,1)}, s32[2,512]{1,0:T(2,128)S(1)}, f32[2,12,512]{2,1,0:T(8...) while((s32[]{:T(128)}, bf16[2,512,2304]{1,2,0:T(8,128)(2,1)}, bf16[2,512,2304]{1,2,0:T(8,128)(2,1)}, ...), condition=%wide.region_12.13_spmd, body=%wide.region_10.12_spmd.sunk | while | flops 2069751808 | bytes 120764512 | solution.py:214
  338.6 6.9 multiply_reduce_fusion.5
  345.5 7.1 multiply_convert_fusion.7
  364.9 6.9 multiply_reduce_fusion.5
  371.8 7.0 multiply_convert_fusion.7
  383.5 6.9 copy.81
  390.5 8.7 fusion.43
  399.8 10.7 %fusion.46 = f32[768,3072]{1,0:T(8,128)} fusion(bf16[1024,3072]{1,0:T(8,128)(2,1)} %copy-done.59, f32[1024,768]{0,1:T(8,128)} %copy-done.7, f32[768]{0:T(1024)S(1)} %copy-done.50, f32[768]{0:T(1024)S(1)} %copy-done.41, f32[1024]{0:T(1024)S(1)} %copy-done.44, f32[1024]{0:T(1024)S(1)} %copy-done.36), kind=kOutput, calls=%fused_computation.114 | convolution fusion | flops 4835770368 | bytes 18888704 | tf_op jit(solution)/shard_map/dot_general | solution.py:46
  412.0 10.2 %fusion.64 = f32[3072,768]{1,0:T(8,128)} fusion(bf16[1024,3072]{1,0:T(8,128)(2,1)} %get-tuple-element.238, bf16[1024,768]{1,0:T(8,128)(2,1)S(1)} %copy-done.16), kind=kOutput, calls=%fused_computation.125 | convolution fusion | flops 4831838208 | bytes 17301504 | tf_op jit(solution)/shard_map/dot_general | solution.py:46
  426.4 7.9 fusion.60
  447.6 80.8 %reduce-scatter.8.cloned.1.call-done = f32[96,2304]{1,0:T(8,128)} async-done(((f32[768,2304]{1,0:T(8,128)}), f32[96,2304]{1,0:T(8,128)}) %reduce-scatter.8.cloned.1.call-update) | async-done | bytes 884752 | tf_op jit(solution)/shard_map/reduce_scatter | solution.py:239
  528.4 164.9 %reduce-scatter.12.cloned.1.call-done = f32[96,3072]{1,0:T(8,128)} async-done(((f32[768,3072]{1,0:T(8,128)}), f32[96,3072]{1,0:T(8,128)}) %reduce-scatter.12.cloned.1.call-update) | async-done | bytes 1179664 | tf_op jit(solution)/shard_map/reduce_scatter | solution.py:207
  693.2 164.8 %reduce-scatter.14.cloned.1.call-done = f32[384,768]{1,0:T(8,128)} async-done(((f32[3072,768]{1,0:T(8,128)}), f32[384,768]{1,0:T(8,128)}) %reduce-scatter.14.cloned.1.call-update) | async-done | bytes 1179664 | tf_op jit(solution)/shard_map/reduce_scatter | solution.py:208
  863.4 59.8 %reduce-scatter.16.cloned.1.call-done = f32[96,12]{1,0:T(8,128)} async-done(((f32[768,12]{1,0:T(8,128)}), f32[96,12]{1,0:T(8,128)}) %reduce-scatter.16.cloned.1.call-update) | async-done | bytes 4624
  930.5 69.2 %all-reduce.3.cloned.1.call-done = (f32[96,2304]{1,0:T(8,128)}, f32[96,768]{1,0:T(8,128)}, f32[96,3072]{1,0:T(8,128)}, f32[384,768]{1,0:T(8,128)}) async-done(((f32[96,2304]{1,0:T(8,128)}, f32[96,768]{1,0:T(8,128)}, f32[96,3072]{1,0:T(8,128)}, f32[384,768]{1,0:T(8,128)}), (f32[96,2304]{1,0:T(8,128)}, f32[96,768]{1,0:T(8,128)}, f32[96,3072]{1,0:T(8,128)}, f32[384,768]{1,0:T(8,128)})) %all-reduce.3.cloned.1.call-update) | async-done | bytes 3538960 | tf_op jit(solution)/shard_map/psum | solution.py:243
  (269 shorter events, 162.2 us)
Async XLA Ops:
  7.2 71.1 %all-gather.5.cloned.1.call-start = ((), (), s32[]{:S(2)}) async-start(), calls=%async_computation.5 | async-start | bytes 3981312 | tf_op jit(solution)/shard_map/all_gather | solution.py:152
  9.4 111.6 %all-gather.7.cloned.1.call-start = ((), (), s32[]{:S(2)}) async-start(), calls=%async_computation.6 | async-start | bytes 1327104 | tf_op jit(solution)/shard_map/all_gather | solution.py:153
  11.1 190.7 %all-gather.9.cloned.1.call-start = ((), (), s32[]{:S(2)}) async-start(), calls=%async_computation.7 | async-start | bytes 5308416 | tf_op jit(solution)/shard_map/all_gather | solution.py:154
  12.1 270.1 %all-gather.11.cloned.1.call-start = ((), (), s32[]{:S(2)}) async-start(), calls=%async_computation.8 | async-start | bytes 5308416 | tf_op jit(solution)/shard_map/all_gather | solution.py:155
  12.2 12.5 %collective-permute-start.1 = (bf16[96,12]{0,1:T(8,128)(2,1)S(1)}, bf16[96,12]{0,1:T(8,128)(2,1)S(1)}, u32[]{:S(2)}, u32[]{:S(2)}) collective-permute-start(bf16[96,12]{0,1:T(8,128)(2,1)S(1)} %convert_element_type.92), channel_id=1, source_target_pairs={{0,7},{1,0},{2,1},{3,2},{4,3},{5,4},{6,5},{7,6},{8,15},{9,8},{10,9... | collective-permute-start | bytes 6920 | tf_op jit(solution)/shard_map/ppermute | solution.py:31
  18.2 6.4 collective-permute-start
  19.1 428.5 %reduce-scatter.10.cloned.1.call-start = ((), (), s32[]{:S(2)}) async-start(), calls=%async_computation.10 | async-start | bytes 2654208 | tf_op jit(solution)/shard_map/reduce_scatter | solution.py:240
  20.9 100.1 %copy-start = (bf16[1024,768]{0,1:T(8,128)(2,1)}, bf16[1024,768]{0,1:T(8,128)(2,1)S(1)}, u32[]{:S(2)}) copy-start(bf16[1024,768]{0,1:T(8,128)(2,1)S(1)} %copy.73) | copy-start | bytes 4718596
  24.6 6.5 collective-permute-start.2
  24.6 6.5 collective-permute-start.3
  31.2 6.5 collective-permute-start.4
  31.2 10.6 %collective-permute-start.5 = (bf16[96,12]{0,1:T(8,128)(2,1)S(1)}, bf16[96,12]{0,1:T(8,128)(2,1)S(1)}, u32[]{:S(2)}, u32[]{:S(2)}) collective-permute-start(bf16[96,12]{0,1:T(8,128)(2,1)S(1)} %collective-permute-done.3), channel_id=1, source_target_pairs={{0,7},{1,0},{2,1},{3,2},{4,3},{5,4},{6,5},{7,6},{8,15},{9,8},{10,9... | collective-permute-start | bytes 6920 | tf_op jit(solution)/shard_map/ppermute | solution.py:31
  37.7 6.3 collective-permute-start.6
  124.4 77.4 %copy-start.40 = (f32[768]{0:T(1024)S(1)}, f32[768]{0:T(1024)}, u32[]{:S(2)}) copy-start(f32[768]{0:T(1024)} %get-tuple-element.170) | copy-start | bytes 9220
  124.4 77.4 %copy-start.46 = (f32[3072]{0:T(1024)S(1)}, f32[3072]{0:T(1024)}, u32[]{:S(2)}) copy-start(f32[3072]{0:T(1024)} %add.308) | copy-start | bytes 36868
  124.5 187.7 %copy-start.35 = (f32[1024]{0:T(1024)}, f32[1024]{0:T(1024)S(1)}, u32[]{:S(2)}) copy-start(f32[1024]{0:T(1024)S(1)} %broadcast_multiply_fusion) | copy-start | bytes 12292
  126.5 185.7 %copy-start.43 = (f32[1024]{0:T(1024)}, f32[1024]{0:T(1024)S(1)}, u32[]{:S(2)}) copy-start(f32[1024]{0:T(1024)S(1)} %fusion.42) | copy-start | bytes 12292
  201.9 80.3 %copy-start.15 = (bf16[1024,768]{1,0:T(8,128)(2,1)S(1)}, bf16[1024,768]{1,0:T(8,128)(2,1)}, u32[]{:S(2)}) copy-start(bf16[1024,768]{1,0:T(8,128)(2,1)} %param.23) | copy-start | bytes 4718596
  328.2 200.2 %reduce-scatter.8.cloned.1.call-start = ((), (), s32[]{:S(2)}) async-start(), calls=%async_computation.9 | async-start | bytes 7962624 | tf_op jit(solution)/shard_map/reduce_scatter | solution.py:239
  399.2 294.1 %reduce-scatter.12.cloned.1.call-start = ((), (), s32[]{:S(2)}) async-start(), calls=%async_computation.11 | async-start | bytes 10616832 | tf_op jit(solution)/shard_map/reduce_scatter | solution.py:207
  410.6 447.4 %reduce-scatter.14.cloned.1.call-start = ((), (), s32[]{:S(2)}) async-start(), calls=%async_computation.12 | async-start | bytes 10616832 | tf_op jit(solution)/shard_map/reduce_scatter | solution.py:208
  422.2 501.0 %reduce-scatter.16.cloned.1.call-start = ((), (), s32[]{:S(2)}) async-start(), calls=%async_computation.13 | async-start | bytes 442368
  447.5 552.1 %all-reduce.3.cloned.1.call-start = ((), (), s32[]{:S(2)}) async-start(), calls=%async_computation.14 | async-start | bytes 7077888 | tf_op jit(solution)/shard_map/psum | solution.py:243
  861.1 138.6 %copy-start.17 = (f32[96,768]{1,0:T(8,128)S(1)}, f32[96,768]{1,0:T(8,128)}, u32[]{:S(2)}) copy-start(f32[96,768]{1,0:T(8,128)} %param.28) | copy-start | bytes 884740
  (53 other events, 709.9 us)
Sparse Core Ops, SparseCore 0:
  10.8 67.5 all-gather.4
  81.1 39.8 all-gather.6
  123.8 78.0 all-gather.8
  204.5 77.6 all-gather.10
  328.3 68.0 reduce-scatter.9
  400.0 128.3 reduce-scatter.7
  532.0 161.2 reduce-scatter.11
  696.8 161.1 reduce-scatter.13
  861.9 61.2 reduce-scatter.15
  925.7 73.9 all-reduce.2
